TPU v7x, 32 devices: a whole 2x2x4 slice. The times are simulated.
32 devices in a mesh: dp: 8 (over y, x, core), mp: 4 (over z).
Axes of the slice: x: 2, y: 2, z: 4, core: 2. Of those that a mesh axis runs over, the one named last changes fastest.
Arguments:
- tokens: bfloat16 [8192, 5120], P('dp'), may hold values from -6 to 6
- norm_gain: bfloat16 [5120], replicated, may hold values from 0.099609375 to 1.8984375
- w_query: bfloat16 [5120, 5120], P('dp', 'mp'), may hold values from -0.078125 to 0.078125
- b_query: bfloat16 [5120], P('mp'), may hold values from -3 to 3
- keyvalue_weight: bfloat16 [5120, 2, 1024], P('dp', None, 'mp'), may hold values from -0.078125 to 0.078125
- b_keyval: bfloat16 [2, 1024], P(None, 'mp'), may hold values from -3 to 3
- w_out: bfloat16 [5120, 5120], P('mp', 'dp'), may hold values from -0.5 to 0.5
- kv_pool: bfloat16 [2, 512, 64, 1024], P(None, 'dp', None, 'mp'), may hold values from -64 to 64
- page_owner: int32 [8, 16], replicated, may hold values from 0 to 7, as said below
- page_index: int32 [8, 16], replicated, may hold values from 0 to 63
- prefix_pages: int32 [8], replicated, may hold values from 10 to 16, as said below
- prompt_device: int32 [8], replicated, may hold values from 0 to 7, each once
Outputs:
- attn_out: bfloat16 [8192, 5120], P('dp', 'mp')
Inputs may be any that keep to these rules, and one draw needn't show every extreme that they name: `page_owner`: slots at or beyond a prompt's prefix_pages are unused. Of one prompt's used slots at most 2 name the same owner, and some prompt has exactly 2 used slots with one owner. `prefix_pages`: some prompt has 16 used slots.
All inputs are finite; a program needn't handle non-finite values.
Results may differ from a plain program's by a relative error of at most 0.014.
The roundings to bfloat16 on the way count: a program that leaves them out, or rounds other values in their place, can miss the bound.
Values may be sent and summed in bfloat16 or wider, within the bound.
A program may use at most 192 MiB of HBM per device.

v0:
```python
import functools
import math

import jax
import jax.numpy as jnp
from jax import lax
from jax.experimental import pallas as pl
from jax.experimental.pallas import tpu as pltpu
from jax.sharding import PartitionSpec as P


HD = 128
CAP = 2
ROW_PARTS = 2


rope_theta = 1000000.0
norm_eps = 1e-06
masked_score = -1e30


def rms_normed(rows, norm_gain):
    values = rows.astype(jnp.float32)
    inverse = lax.rsqrt(jnp.mean(values * values, axis=-1, keepdims=True) + norm_eps)
    return (values * inverse * norm_gain.astype(jnp.float32)).astype(jnp.bfloat16)


def rotary_tables(positions):
    half_dim = HD // 2
    frequency = rope_theta ** (-jnp.arange(half_dim, dtype=jnp.float32) * 2.0 / HD)
    angles = positions.astype(jnp.float32)[:, None] * frequency[None, :]
    cosine = jnp.cos(angles)
    sine = jnp.sin(angles)
    return (
        jnp.concatenate([cosine, cosine], axis=-1),
        jnp.concatenate([-sine, sine], axis=-1),
    )


def attention_kernel(block, prev_len, *refs):
    q_ref, k_ref, v_ref, cos_ref, sin_ref, bias_ref, kp_ref, vp_ref = refs[:8]
    refs = refs[8:]
    if prev_len:
        k_prev_ref, v_prev_ref = refs[:2]
        refs = refs[2:]
    o_ref, k_out, v_out = refs
    cosine = cos_ref[...]
    sine = sin_ref[...]

    def rotate(x):
        return (x * cosine + pltpu.roll(x, HD // 2, 1) * sine).astype(jnp.bfloat16)

    @pl.when(pl.program_id(0) == 0)
    def _():
        k_out[...] = rotate(k_ref[...])
        v_out[...] = v_ref[...].astype(jnp.bfloat16)

    query = rotate(q_ref[...])
    factor = HD ** (-0.5) * math.log2(math.e)
    rows = query.shape[0]
    ids = lax.broadcasted_iota(jnp.int32, (block, block), 0)
    keys_id = lax.broadcasted_iota(jnp.int32, (block, block), 1)

    def scores(q, k):
        return lax.dot_general(q, k, (((1,), (1,)), ((), ())), preferred_element_type=jnp.float32)

    for begin in range(0, rows, block):
        q = query[begin : begin + block]
        parts = [(scores(q, kp_ref[0]) + bias_ref[...], vp_ref[0])]
        if prev_len:
            parts.append((scores(q, k_prev_ref[...]), v_prev_ref[...]))
        if begin:
            parts.append((scores(q, k_out[0:begin, :]), v_out[0:begin, :]))
        diagonal = scores(q, k_out[begin : begin + block, :])
        diagonal = jnp.where(keys_id <= ids, diagonal, masked_score)
        parts.append((diagonal, v_out[begin : begin + block, :]))
        top = functools.reduce(
            jnp.maximum, [jnp.max(s, axis=-1, keepdims=True) for s, _ in parts]
        )
        total = None
        out = None
        for s, v in parts:
            raised = jnp.exp2((s - top) * factor)
            row_sum = jnp.sum(raised, axis=-1, keepdims=True)
            term = jnp.dot(raised.astype(jnp.bfloat16), v, preferred_element_type=jnp.float32)
            total = row_sum if total is None else total + row_sum
            out = term if out is None else out + term
        o_ref[begin : begin + block, :] = (out / total).astype(jnp.bfloat16)


def attention(group, qkv, cosine, sine, bias, arrived, prev, per_group):
    rows = qkv.shape[0]
    cached_len = arrived.shape[1]
    block = math.gcd(256, rows)
    const = lambda shape, index: pl.BlockSpec(shape, lambda h: index)
    in_specs = [
        pl.BlockSpec((rows, HD), lambda h: (0, h)),
        const((rows, HD), (0, per_group)),
        const((rows, HD), (0, per_group + 1)),
        const((rows, HD), (0, 0)),
        const((rows, HD), (0, 0)),
        const((1, cached_len), (0, 0)),
        const((1, cached_len, HD), (0, 0, group)),
        const((1, cached_len, HD), (1, 0, group)),
    ]
    operands = [qkv, qkv, qkv, cosine, sine, bias, arrived, arrived]
    prev_len = 0
    if prev is not None:
        prev_len = prev[0].shape[0]
        in_specs += [const((prev_len, HD), (0, 0))] * 2
        operands += list(prev)
    keys = cached_len + prev_len + rows
    return pl.pallas_call(
        functools.partial(attention_kernel, block, prev_len),
        grid=(per_group,),
        in_specs=in_specs,
        out_specs=[
            pl.BlockSpec((rows, HD), lambda h: (0, h)),
            const((rows, HD), (0, 0)),
            const((rows, HD), (0, 0)),
        ],
        out_shape=[
            jax.ShapeDtypeStruct((rows, per_group * HD), jnp.bfloat16),
            jax.ShapeDtypeStruct((rows, HD), jnp.bfloat16),
            jax.ShapeDtypeStruct((rows, HD), jnp.bfloat16),
        ],
        compiler_params=pltpu.CompilerParams(
            dimension_semantics=("arbitrary",), vmem_limit_bytes=40 * 1024 * 1024
        ),
        cost_estimate=pl.CostEstimate(
            flops=8 * per_group * rows * keys * HD,
            bytes_accessed=6 * rows * (per_group + 2) * HD,
            transcendentals=per_group * rows * keys,
        ),
    )(*operands)


def exchange(x, axis, split_axis, concat_axis):
    size = lax.axis_size(axis)
    me = lax.axis_index(axis)
    width = x.shape[split_axis] // size
    span = x.shape[concat_axis]
    shape = list(x.shape)
    shape[split_axis] = width
    shape[concat_axis] = span * size
    result = jnp.zeros(shape, x.dtype)
    for s in range(size):
        target = lax.rem(me + s, size)
        source = lax.rem(me - s + size, size)
        piece = lax.dynamic_slice_in_dim(x, target * width, width, split_axis)
        if s:
            piece = lax.ppermute(piece, axis, [(i, (i + s) % size) for i in range(size)])
        result = lax.dynamic_update_slice_in_dim(result, piece, source * span, concat_axis)
    return result


def layer(
    tokens,
    norm_gain,
    w_query,
    b_query,
    keyvalue_weight,
    b_keyval,
    w_out,
    kv_pool,
    page_owner,
    page_index,
    prefix_pages,
    prompt_device,
):
    groups = lax.axis_size("dp")
    planes = lax.axis_size("mp")
    my_group = lax.axis_index("dp")
    my_plane = lax.axis_index("mp")
    seq_rows = tokens.shape[0]
    width_kv = keyvalue_weight.shape[2]
    kv_local = width_kv // HD
    heads_local = w_query.shape[1] // HD
    per_group = heads_local // kv_local
    page_len = kv_pool.shape[2]
    max_pages = page_owner.shape[1]
    group_ids = jnp.arange(groups, dtype=jnp.int32)

    width_q = per_group * HD
    gathered = []
    biases = []
    for g in range(kv_local):
        piece = jnp.concatenate(
            [
                w_query[:, g * width_q : (g + 1) * width_q],
                keyvalue_weight[:, 0, g * HD : (g + 1) * HD],
                keyvalue_weight[:, 1, g * HD : (g + 1) * HD],
            ],
            axis=1,
        )
        gathered.append(lax.all_gather(piece, "dp", axis=0, tiled=True))
        biases.append(
            jnp.concatenate(
                [
                    b_query[g * width_q : (g + 1) * width_q],
                    b_keyval[0, g * HD : (g + 1) * HD],
                    b_keyval[1, g * HD : (g + 1) * HD],
                ]
            ).astype(jnp.float32)
        )

    slot_prompt = jnp.sum(
        jnp.where(prompt_device[None, :] == group_ids[:, None], group_ids[None, :], 0), axis=1
    )
    owners_all = jnp.take(page_owner, slot_prompt, axis=0)
    index_all = jnp.take(page_index, slot_prompt, axis=0)
    length_all = jnp.take(prefix_pages, slot_prompt, axis=0)
    slot_ids = jnp.arange(max_pages, dtype=jnp.int32)
    places = jnp.arange(CAP, dtype=jnp.int32)
    used = slot_ids[None, :] < length_all[:, None]
    mine = used & (owners_all == my_group)
    rank = jnp.cumsum(mine.astype(jnp.int32), axis=1) - 1
    chosen = mine[:, None, :] & (rank[:, None, :] == places[None, :, None])
    send_index = jnp.sum(jnp.where(chosen, index_all[:, None, :], 0), axis=2)
    outgoing = jnp.take(kv_pool, send_index.reshape(-1), axis=1).reshape(
        2, groups, CAP, page_len, width_kv
    )
    arrived = lax.all_to_all(outgoing, "dp", split_axis=1, concat_axis=1, tiled=True)
    my_owners = jnp.take(owners_all, my_group, axis=0)
    my_length = jnp.take(length_all, my_group, axis=0)
    my_used = slot_ids < my_length
    counts = jnp.sum(
        ((my_owners[None, :] == group_ids[:, None]) & my_used[None, :]).astype(jnp.int32), axis=1
    )
    page_live = (places[None, :] < counts[:, None]).reshape(-1)
    cached_len = page_live.shape[0] * page_len
    arrived = arrived.reshape(2, cached_len, width_kv)
    bias = jnp.where(jnp.repeat(page_live, page_len), 0.0, masked_score).astype(jnp.float32)[None]

    normed = rms_normed(tokens, norm_gain)
    arrived, w_out = lax.optimization_barrier((arrived, w_out))
    out_rows = exchange(w_out, "dp", 0, 1)
    out_rows = exchange(out_rows, "mp", 1, 0)
    out_weight = lax.all_gather(out_rows, "dp", axis=0, tiled=True)
    out_cols = out_weight.shape[1]
    out_weight = out_weight.reshape(groups, planes, -1, out_cols)
    cosine, sine = rotary_tables(
        my_length * page_len + jnp.arange(seq_rows, dtype=jnp.int32)
    )
    part = seq_rows // ROW_PARTS
    held = [[[] for _ in range(ROW_PARTS)] for _ in range(planes)]
    for g in range(kv_local):
        prev = None
        for r in range(ROW_PARTS):
            rows = slice(r * part, (r + 1) * part)
            qkv = (
                jnp.dot(normed[rows], gathered[g], preferred_element_type=jnp.float32)
                + biases[g]
            )
            attended, keys, values = attention(
                g, qkv, cosine[rows], sine[rows], bias, arrived, prev, per_group
            )
            if prev is None:
                prev = (keys, values)
            else:
                prev = (
                    jnp.concatenate([prev[0], keys], axis=0),
                    jnp.concatenate([prev[1], values], axis=0),
                )
            held[0][r].append(attended)
            for s in range(1, planes):
                held[s][r].append(
                    lax.ppermute(
                        attended, "mp", [(i, (i + s) % planes) for i in range(planes)]
                    )
                )
    weights = []
    for s in range(planes):
        source = lax.rem(my_plane - s + planes, planes)
        rows_of = lax.dynamic_index_in_dim(out_weight, source, axis=1, keepdims=False)
        weights.append(rows_of.reshape(-1, out_cols))
    outputs = []
    for r in range(ROW_PARTS):
        total = None
        for s in range(planes):
            head_partial = None
            for g in range(kv_local):
                term = jnp.dot(
                    held[s][r][g],
                    weights[s][g * width_q : (g + 1) * width_q],
                    preferred_element_type=jnp.float32,
                )
                head_partial = term if head_partial is None else term + head_partial
            head_partial = head_partial.astype(jnp.bfloat16).astype(jnp.float32)
            total = head_partial if total is None else total + head_partial
        outputs.append(total.astype(jnp.bfloat16))
    return jnp.concatenate(outputs, axis=0)


def solution(mesh):
    return jax.shard_map(
        layer,
        mesh=mesh,
        in_specs=(
            P("dp", None),
            P(),
            P("dp", "mp"),
            P("mp"),
            P("dp", None, "mp"),
            P(None, "mp"),
            P("mp", "dp"),
            P(None, "dp", None, "mp"),
            P(),
            P(),
            P(),
            P(),
        ),
        out_specs=P("dp", "mp"),
        check_vma=False,
    )
```

profile of v0, /device:TPU:0, one launch (start us, length us, event | category | flops | bytes accessed | tf_op | source)
XLA Modules:
  0.0 435.2 jit_solution(10346001370949771411)
XLA Ops:
  18.8 5.2 %all-to-all-start = ((bf16[2,8,2,64,256]{4,3,2,0,1:T(8,128)(2,1)}), bf16[2,8,2,64,256]{4,3,2,0,1:T(8,128)(2,1)S(1)}, u32[]{:S(2)}, u32[]{:S(2)}) async-start(bf16[2,8,2,64,256]{4,3,2,0,1:T(8,128)(2,1)} %copy.42), calls=%async_computation | async-start | bytes 2097152 | tf_op jit(solution)/shard_map/all_to_all | solution.py:223
  24.1 24.3 %all-to-all-done = bf16[2,8,2,64,256]{4,3,2,0,1:T(8,128)(2,1)S(1)} async-done(((bf16[2,8,2,64,256]{4,3,2,0,1:T(8,128)(2,1)}), bf16[2,8,2,64,256]{4,3,2,0,1:T(8,128)(2,1)S(1)}, u32[]{:S(2)}, u32[]{:S(2)}) %all-to-all-start) | async-done | bytes 1048608 | tf_op jit(solution)/shard_map/all_to_all | solution.py:223
  54.1 6.8 %collective-permute-done = bf16[160,640]{1,0:T(8,128)(2,1)S(1)} collective-permute-done((bf16[160,640]{1,0:T(8,128)(2,1)}, bf16[160,640]{1,0:T(8,128)(2,1)S(1)}, u32[]{:S(2)}, u32[]{:S(2)}) %collective-permute-start) | collective-permute-done | bytes 204832 | tf_op jit(solution)/shard_map/ppermute | solution.py:152
  63.2 5.8 %collective-permute-start.6 = (bf16[160,640]{1,0:T(8,128)(2,1)S(1)}, bf16[160,640]{1,0:T(8,128)(2,1)S(1)}, u32[]{:S(2)}, u32[]{:S(2)}) collective-permute-start(bf16[160,640]{1,0:T(8,128)(2,1)S(1)} %get-tuple-element.67), channel_id=1, source_target_pairs={{0,28},{4,0},{8,4},{12,8},{16,12},{20,16},{24,20},{28,24},{1,29},{... | collective-permute-start | bytes 614408 | tf_op jit(solution)/shard_map/ppermute | solution.py:152
  72.6 7.1 %collective-permute-done.4 = bf16[160,640]{1,0:T(8,128)(2,1)S(1)} collective-permute-done((bf16[160,640]{1,0:T(8,128)(2,1)}, bf16[160,640]{1,0:T(8,128)(2,1)S(1)}, u32[]{:S(2)}, u32[]{:S(2)}) %collective-permute-start.4) | collective-permute-done | bytes 204832 | tf_op jit(solution)/shard_map/ppermute | solution.py:152
  92.3 6.7 %collective-permute-done.7 = bf16[160,1280]{1,0:T(8,128)(2,1)S(1)} collective-permute-done((bf16[160,1280]{1,0:T(8,128)(2,1)}, bf16[160,1280]{1,0:T(8,128)(2,1)S(1)}, u32[]{:S(2)}, u32[]{:S(2)}) %collective-permute-start.7) | collective-permute-done | bytes 409632 | tf_op jit(solution)/shard_map/ppermute | solution.py:152
  99.8 19.0 %collective-permute-done.8 = bf16[160,1280]{1,0:T(8,128)(2,1)S(1)} collective-permute-done((bf16[160,1280]{1,0:T(8,128)(2,1)S(1)}, bf16[160,1280]{1,0:T(8,128)(2,1)S(1)}, u32[]{:S(2)}, u32[]{:S(2)}) %collective-permute-start.8) | collective-permute-done | bytes 409632 | tf_op jit(solution)/shard_map/ppermute | solution.py:152
  124.5 6.1 %fusion = f32[1024]{0:T(1024)S(1)} fusion(bf16[1024,5120]{1,0:T(8,128)(2,1)} %param.14), kind=kLoop, calls=%fused_computation.6 | loop fusion | flops 15727616 | bytes 10489856 | tf_op jit(solution)/shard_map/reduce_sum | solution.py:24
  130.6 11.6 %fusion.2 = bf16[1024,5120]{1,0:T(8,128)(2,1)} fusion(bf16[1024,5120]{1,0:T(8,128)(2,1)} %param.14, f32[5120]{0:T(1024)S(1)} %convert_element_type.91, f32[1024]{0:T(1024)S(1)} %add_rsqrt_fusion), kind=kLoop, calls=%fused_computation.8 | loop fusion | flops 20971520 | bytes 20996096 | tf_op jit(solution)/shard_map/convert_element_type | solution.py:25
  142.2 12.3 %fusion.38.refs_0_.refs_1_.refs_2_ = f32[512,896]{1,0:T(8,128)S(1)} fusion(bf16[5120,896]{1,0:T(8,128)(2,1)} %all-gather.8.cloned.1.call-done, bf16[1024,5120]{1,0:T(8,128)(2,1)} %fusion.2, f32[896]{0:T(1024)S(1)} %maximum_convert_fusion.1), kind=kOutput, calls=%fused_computation.51 | convolution fusion | flops 4698079232 | bytes 16256512 | tf_op jit(solution)/shard_map/dot_general | solution.py:252
  154.5 8.2 %shard_map.119 = (bf16[512,640]{1,0:T(8,128)(2,1)S(1)}, bf16[512,128]{1,0:T(8,128)(2,1)S(1)}, bf16[512,128]{1,0:T(8,128)(2,1)S(1)}) custom-call(f32[512,896]{1,0:T(8,128)S(1)} %fusion.38.refs_0_.refs_1_.refs_2_, f32[512,896]{1,0:T(8,128)S(1)} %fusion.38.refs_0_.refs_1_.refs_2_, f32[512,896]{1,0:T(8,128)S(1)} %fusion.38.refs_0_.refs_1_.refs_2_, ...), custom_call_target="tpu_custom_call" | custom-call | flops 4026531840 | bytes 2752512 | tf_op jit(solution)/shard_map/pallas_call | solution.py:113
  162.7 10.8 %fusion.44.refs_0_.refs_1_.refs_2_ = f32[512,896]{1,0:T(8,128)S(1)} fusion(bf16[5120,896]{1,0:T(8,128)(2,1)} %all-gather.8.cloned.1.call-done, bf16[1024,5120]{1,0:T(8,128)(2,1)S(1)} %copy-done.5, f32[896]{0:T(1024)S(1)} %maximum_convert_fusion.1), kind=kOutput, calls=%fused_computation.53 | convolution fusion | flops 4698079232 | bytes 16257024 | tf_op jit(solution)/shard_map/dot_general | solution.py:252
  173.5 10.6 %shard_map.121 = (bf16[512,640]{1,0:T(8,128)(2,1)S(1)}, bf16[512,128]{1,0:T(8,128)(2,1)}, bf16[512,128]{1,0:T(8,128)(2,1)}) custom-call(f32[512,896]{1,0:T(8,128)S(1)} %fusion.44.refs_0_.refs_1_.refs_2_, f32[512,896]{1,0:T(8,128)S(1)} %fusion.44.refs_0_.refs_1_.refs_2_, f32[512,896]{1,0:T(8,128)S(1)} %fusion.44.refs_0_.refs_1_.refs_2_, ...), custom_call_target="tpu_custom_call" | custom-call | flops 5368709120 | bytes 2752512 | tf_op jit(solution)/shard_map/pallas_call | solution.py:113
  184.1 9.5 %collective-permute-start.21 = (bf16[512,640]{1,0:T(8,128)(2,1)S(1)}, bf16[512,640]{1,0:T(8,128)(2,1)}, u32[]{:S(2)}, u32[]{:S(2)}) collective-permute-start(bf16[512,640]{1,0:T(8,128)(2,1)S(1)} %get-tuple-element.25), channel_id=1, source_target_pairs={{0,3},{1,0},{2,1},{3,2},{4,7},{5,4},{6,5},{7,6},{8,11},{9,8},{10,9... | collective-permute-start | bytes 1966088 | tf_op jit(solution)/shard_map/ppermute | solution.py:268
  194.4 14.6 %fusion.35.refs_0_.refs_1_.refs_2_ = f32[512,896]{1,0:T(8,128)S(1)} fusion(bf16[5120,896]{1,0:T(8,128)(2,1)} %all-gather.4.cloned.1.call-done, bf16[1024,5120]{1,0:T(8,128)(2,1)} %fusion.2, f32[896]{0:T(1024)S(1)} %maximum_convert_fusion), kind=kOutput, calls=%fused_computation.50 | convolution fusion | flops 4698079232 | bytes 16256512 | tf_op jit(solution)/shard_map/dot_general | solution.py:252
  209.1 8.2 %shard_map.118 = (bf16[512,640]{1,0:T(8,128)(2,1)S(1)}, bf16[512,128]{1,0:T(8,128)(2,1)S(1)}, bf16[512,128]{1,0:T(8,128)(2,1)S(1)}) custom-call(f32[512,896]{1,0:T(8,128)S(1)} %fusion.35.refs_0_.refs_1_.refs_2_, f32[512,896]{1,0:T(8,128)S(1)} %fusion.35.refs_0_.refs_1_.refs_2_, f32[512,896]{1,0:T(8,128)S(1)} %fusion.35.refs_0_.refs_1_.refs_2_, ...), custom_call_target="tpu_custom_call" | custom-call | flops 4026531840 | bytes 2752512 | tf_op jit(solution)/shard_map/pallas_call | solution.py:113
  217.3 7.9 %fusion.41.refs_0_.refs_1_.refs_2_ = f32[512,896]{1,0:T(8,128)S(1)} fusion(bf16[5120,896]{1,0:T(8,128)(2,1)S(1)} %copy-done.13, bf16[1024,5120]{1,0:T(8,128)(2,1)} %fusion.2, f32[896]{0:T(1024)S(1)} %maximum_convert_fusion), kind=kOutput, calls=%fused_computation.52 | convolution fusion | flops 4698079232 | bytes 16256512 | tf_op jit(solution)/shard_map/dot_general | solution.py:252
  225.2 10.5 %shard_map.120 = (bf16[512,640]{1,0:T(8,128)(2,1)}, bf16[512,128]{1,0:T(8,128)(2,1)}, bf16[512,128]{1,0:T(8,128)(2,1)}) custom-call(f32[512,896]{1,0:T(8,128)S(1)} %fusion.41.refs_0_.refs_1_.refs_2_, f32[512,896]{1,0:T(8,128)S(1)} %fusion.41.refs_0_.refs_1_.refs_2_, f32[512,896]{1,0:T(8,128)S(1)} %fusion.41.refs_0_.refs_1_.refs_2_, ...), custom_call_target="tpu_custom_call" | custom-call | flops 5368709120 | bytes 2752512 | tf_op jit(solution)/shard_map/pallas_call | solution.py:113
  239.5 5.8 %constant_dynamic-slice_fusion.18 = (bf16[4,1,160,1280]{3,2,1,0:T(8,128)(2,1)S(1)}, bf16[4,1,160,1280]{3,2,1,0:T(8,128)(2,1)S(1)}, bf16[4,1,160,1280]{3,2,1,0:T(...) fusion(bf16[8,4,160,1280]{3,2,1,0:T(8,128)(2,1)} %bitcast.89, ...), kind=kLoop, calls=%fused_computation.102 | loop fusion | bytes 26214420 | tf_op jit(solution)/shard_map/slice | solution.py:285
  257.7 37.8 %collective-permute-done.15 = bf16[512,640]{1,0:T(8,128)(2,1)S(1)} collective-permute-done((bf16[512,640]{1,0:T(8,128)(2,1)S(1)}, bf16[512,640]{1,0:T(8,128)(2,1)S(1)}, u32[]{:S(2)}, u32[]{:S(2)}) %collective-permute-start.15) | collective-permute-done | bytes 655392 | tf_op jit(solution)/shard_map/ppermute | solution.py:268
  295.4 14.3 %collective-permute-start.16 = (bf16[512,640]{1,0:T(8,128)(2,1)}, bf16[512,640]{1,0:T(8,128)(2,1)S(1)}, u32[]{:S(2)}, u32[]{:S(2)}) collective-permute-start(bf16[512,640]{1,0:T(8,128)(2,1)} %get-tuple-element.22), channel_id=1, source_target_pairs={{0,1},{1,2},{2,3},{3,0},{4,5},{5,6},{6,7},{7,4},{8,9},{9,10},{10,1... | collective-permute-start | bytes 1966088 | tf_op jit(solution)/shard_map/ppermute | solution.py:268
  310.9 25.9 %collective-permute-start.13 = (bf16[512,640]{1,0:T(8,128)(2,1)S(1)}, bf16[512,640]{1,0:T(8,128)(2,1)S(1)}, u32[]{:S(2)}, u32[]{:S(2)}) collective-permute-start(bf16[512,640]{1,0:T(8,128)(2,1)S(1)} %get-tuple-element.19), channel_id=1, source_target_pairs={{0,2},{1,3},{2,0},{3,1},{4,6},{5,7},{6,4},{7,5},{8,10},{9,11},{10,... | collective-permute-start | bytes 1966088 | tf_op jit(solution)/shard_map/ppermute | solution.py:268
  345.7 48.8 %collective-permute-done.13 = bf16[512,640]{1,0:T(8,128)(2,1)S(1)} collective-permute-done((bf16[512,640]{1,0:T(8,128)(2,1)S(1)}, bf16[512,640]{1,0:T(8,128)(2,1)S(1)}, u32[]{:S(2)}, u32[]{:S(2)}) %collective-permute-start.13) | collective-permute-done | bytes 655392 | tf_op jit(solution)/shard_map/ppermute | solution.py:268
  399.4 23.1 %collective-permute-done.12 = bf16[512,640]{1,0:T(8,128)(2,1)S(1)} collective-permute-done((bf16[512,640]{1,0:T(8,128)(2,1)S(1)}, bf16[512,640]{1,0:T(8,128)(2,1)S(1)}, u32[]{:S(2)}, u32[]{:S(2)}) %collective-permute-start.12) | collective-permute-done | bytes 655392 | tf_op jit(solution)/shard_map/ppermute | solution.py:268
  (150 shorter events, 79.5 us)
Async XLA Ops:
  6.5 135.6 %all-gather.8.cloned.1.call-start = ((), (), s32[]{:S(2)}) async-start(), calls=%async_computation.3 | async-start | bytes 10321920 | tf_op jit(solution)/shard_map/all_gather | solution.py:196
  10.5 183.9 %all-gather.4.cloned.1.call-start = ((), (), s32[]{:S(2)}) async-start(), calls=%async_computation.1 | async-start | bytes 10321920 | tf_op jit(solution)/shard_map/all_gather | solution.py:196
  18.8 29.7 %all-to-all-start = ((bf16[2,8,2,64,256]{4,3,2,0,1:T(8,128)(2,1)}), bf16[2,8,2,64,256]{4,3,2,0,1:T(8,128)(2,1)S(1)}, u32[]{:S(2)}, u32[]{:S(2)}) async-start(bf16[2,8,2,64,256]{4,3,2,0,1:T(8,128)(2,1)} %copy.42), calls=%async_computation | async-start | bytes 2097152 | tf_op jit(solution)/shard_map/all_to_all | solution.py:223
  24.0 215.6 %all-gather.6.cloned.1.call-start = ((), (), s32[]{:S(2)}) async-start(), calls=%async_computation.2 | async-start | bytes 14745600 | tf_op jit(solution)/shard_map/all_gather | solution.py:239
  50.8 12.4 %collective-permute-start.1 = (bf16[160,640]{1,0:T(8,128)(2,1)}, bf16[160,640]{1,0:T(8,128)(2,1)S(1)}, u32[]{:S(2)}, u32[]{:S(2)}) collective-permute-start(bf16[160,640]{1,0:T(8,128)(2,1)} %get-tuple-element.72), channel_id=1, source_target_pairs={{0,8},{4,12},{8,16},{12,20},{16,24},{20,28},{24,0},{28,4},{1,9},{5... | collective-permute-start | bytes 614408 | tf_op jit(solution)/shard_map/ppermute | solution.py:152
  50.9 21.5 %collective-permute-start.2 = (bf16[160,640]{1,0:T(8,128)(2,1)}, bf16[160,640]{1,0:T(8,128)(2,1)S(1)}, u32[]{:S(2)}, u32[]{:S(2)}) collective-permute-start(bf16[160,640]{1,0:T(8,128)(2,1)} %get-tuple-element.71), channel_id=1, source_target_pairs={{0,12},{4,16},{8,20},{12,24},{16,28},{20,0},{24,4},{28,8},{1,13},{... | collective-permute-start | bytes 614408 | tf_op jit(solution)/shard_map/ppermute | solution.py:152
  52.9 19.7 %collective-permute-start.3 = (bf16[160,640]{1,0:T(8,128)(2,1)}, bf16[160,640]{1,0:T(8,128)(2,1)S(1)}, u32[]{:S(2)}, u32[]{:S(2)}) collective-permute-start(bf16[160,640]{1,0:T(8,128)(2,1)} %get-tuple-element.70), channel_id=1, source_target_pairs={{0,16},{4,20},{8,24},{12,28},{16,0},{20,4},{24,8},{28,12},{1,17},{... | collective-permute-start | bytes 614408 | tf_op jit(solution)/shard_map/ppermute | solution.py:152
  54.1 25.6 %collective-permute-start.4 = (bf16[160,640]{1,0:T(8,128)(2,1)}, bf16[160,640]{1,0:T(8,128)(2,1)S(1)}, u32[]{:S(2)}, u32[]{:S(2)}) collective-permute-start(bf16[160,640]{1,0:T(8,128)(2,1)} %get-tuple-element.69), channel_id=1, source_target_pairs={{0,20},{4,24},{8,28},{12,0},{16,4},{20,8},{24,12},{28,16},{1,21},{... | collective-permute-start | bytes 614408 | tf_op jit(solution)/shard_map/ppermute | solution.py:152
  60.9 19.0 %collective-permute-start.5 = (bf16[160,640]{1,0:T(8,128)(2,1)S(1)}, bf16[160,640]{1,0:T(8,128)(2,1)S(1)}, u32[]{:S(2)}, u32[]{:S(2)}) collective-permute-start(bf16[160,640]{1,0:T(8,128)(2,1)S(1)} %get-tuple-element.68), channel_id=1, source_target_pairs={{0,24},{4,28},{8,0},{12,4},{16,8},{20,12},{24,16},{28,20},{1,25},{... | collective-permute-start | bytes 614408 | tf_op jit(solution)/shard_map/ppermute | solution.py:152
  63.2 21.5 %collective-permute-start.6 = (bf16[160,640]{1,0:T(8,128)(2,1)S(1)}, bf16[160,640]{1,0:T(8,128)(2,1)S(1)}, u32[]{:S(2)}, u32[]{:S(2)}) collective-permute-start(bf16[160,640]{1,0:T(8,128)(2,1)S(1)} %get-tuple-element.67), channel_id=1, source_target_pairs={{0,28},{4,0},{8,4},{12,8},{16,12},{20,16},{24,20},{28,24},{1,29},{... | collective-permute-start | bytes 614408 | tf_op jit(solution)/shard_map/ppermute | solution.py:152
  88.4 30.4 %collective-permute-start.8 = (bf16[160,1280]{1,0:T(8,128)(2,1)S(1)}, bf16[160,1280]{1,0:T(8,128)(2,1)S(1)}, u32[]{:S(2)}, u32[]{:S(2)}) collective-permute-start(bf16[160,1280]{1,0:T(8,128)(2,1)S(1)} %get-tuple-element.64), channel_id=1, source_target_pairs={{0,2},{1,3},{2,0},{3,1},{4,6},{5,7},{6,4},{7,5},{8,10},{9,11},{10,... | collective-permute-start | bytes 1228808 | tf_op jit(solution)/shard_map/ppermute | solution.py:152
  90.8 28.8 %collective-permute-start.9 = (bf16[160,1280]{1,0:T(8,128)(2,1)S(1)}, bf16[160,1280]{1,0:T(8,128)(2,1)S(1)}, u32[]{:S(2)}, u32[]{:S(2)}) collective-permute-start(bf16[160,1280]{1,0:T(8,128)(2,1)S(1)} %get-tuple-element.63), channel_id=1, source_target_pairs={{0,3},{1,0},{2,1},{3,2},{4,7},{5,4},{6,5},{7,6},{8,11},{9,8},{10,9... | collective-permute-start | bytes 1228808 | tf_op jit(solution)/shard_map/ppermute | solution.py:152
  184.1 67.3 %collective-permute-start.21 = (bf16[512,640]{1,0:T(8,128)(2,1)S(1)}, bf16[512,640]{1,0:T(8,128)(2,1)}, u32[]{:S(2)}, u32[]{:S(2)}) collective-permute-start(bf16[512,640]{1,0:T(8,128)(2,1)S(1)} %get-tuple-element.25), channel_id=1, source_target_pairs={{0,3},{1,0},{2,1},{3,2},{4,7},{5,4},{6,5},{7,6},{8,11},{9,8},{10,9... | collective-permute-start | bytes 1966088 | tf_op jit(solution)/shard_map/ppermute | solution.py:268
  193.5 144.5 %collective-permute-start.19 = (bf16[512,640]{1,0:T(8,128)(2,1)S(1)}, bf16[512,640]{1,0:T(8,128)(2,1)}, u32[]{:S(2)}, u32[]{:S(2)}) collective-permute-start(bf16[512,640]{1,0:T(8,128)(2,1)S(1)} %get-tuple-element.25), channel_id=1, source_target_pairs={{0,2},{1,3},{2,0},{3,1},{4,6},{5,7},{6,4},{7,5},{8,10},{9,11},{10,... | collective-permute-start | bytes 1966088 | tf_op jit(solution)/shard_map/ppermute | solution.py:268
  235.8 19.8 %collective-permute-start.20 = (bf16[512,640]{1,0:T(8,128)(2,1)}, bf16[512,640]{1,0:T(8,128)(2,1)S(1)}, u32[]{:S(2)}, u32[]{:S(2)}) collective-permute-start(bf16[512,640]{1,0:T(8,128)(2,1)} %get-tuple-element.22), channel_id=1, source_target_pairs={{0,3},{1,0},{2,1},{3,2},{4,7},{5,4},{6,5},{7,6},{8,11},{9,8},{10,9... | collective-permute-start | bytes 1966088 | tf_op jit(solution)/shard_map/ppermute | solution.py:268
  235.8 104.6 %collective-permute-start.18 = (bf16[512,640]{1,0:T(8,128)(2,1)}, bf16[512,640]{1,0:T(8,128)(2,1)S(1)}, u32[]{:S(2)}, u32[]{:S(2)}) collective-permute-start(bf16[512,640]{1,0:T(8,128)(2,1)} %get-tuple-element.22), channel_id=1, source_target_pairs={{0,2},{1,3},{2,0},{3,1},{4,6},{5,7},{6,4},{7,5},{8,10},{9,11},{10,... | collective-permute-start | bytes 1966088 | tf_op jit(solution)/shard_map/ppermute | solution.py:268
  237.6 158.3 %collective-permute-start.17 = (bf16[512,640]{1,0:T(8,128)(2,1)S(1)}, bf16[512,640]{1,0:T(8,128)(2,1)}, u32[]{:S(2)}, u32[]{:S(2)}) collective-permute-start(bf16[512,640]{1,0:T(8,128)(2,1)S(1)} %get-tuple-element.25), channel_id=1, source_target_pairs={{0,1},{1,2},{2,3},{3,0},{4,5},{5,6},{6,7},{7,4},{8,9},{9,10},{10,1... | collective-permute-start | bytes 1966088 | tf_op jit(solution)/shard_map/ppermute | solution.py:268
  251.3 44.1 %collective-permute-start.15 = (bf16[512,640]{1,0:T(8,128)(2,1)S(1)}, bf16[512,640]{1,0:T(8,128)(2,1)S(1)}, u32[]{:S(2)}, u32[]{:S(2)}) collective-permute-start(bf16[512,640]{1,0:T(8,128)(2,1)S(1)} %get-tuple-element.19), channel_id=1, source_target_pairs={{0,3},{1,0},{2,1},{3,2},{4,7},{5,4},{6,5},{7,6},{8,11},{9,8},{10,9... | collective-permute-start | bytes 1966088 | tf_op jit(solution)/shard_map/ppermute | solution.py:268
  255.6 55.3 %collective-permute-start.14 = (bf16[512,640]{1,0:T(8,128)(2,1)S(1)}, bf16[512,640]{1,0:T(8,128)(2,1)S(1)}, u32[]{:S(2)}, u32[]{:S(2)}) collective-permute-start(bf16[512,640]{1,0:T(8,128)(2,1)S(1)} %copy-done.3), channel_id=1, source_target_pairs={{0,3},{1,0},{2,1},{3,2},{4,7},{5,4},{6,5},{7,6},{8,11},{9,8},{10,9... | collective-permute-start | bytes 1966088 | tf_op jit(solution)/shard_map/ppermute | solution.py:268
  295.4 128.3 %collective-permute-start.16 = (bf16[512,640]{1,0:T(8,128)(2,1)}, bf16[512,640]{1,0:T(8,128)(2,1)S(1)}, u32[]{:S(2)}, u32[]{:S(2)}) collective-permute-start(bf16[512,640]{1,0:T(8,128)(2,1)} %get-tuple-element.22), channel_id=1, source_target_pairs={{0,1},{1,2},{2,3},{3,0},{4,5},{5,6},{6,7},{7,4},{8,9},{9,10},{10,1... | collective-permute-start | bytes 1966088 | tf_op jit(solution)/shard_map/ppermute | solution.py:268
  310.9 83.6 %collective-permute-start.13 = (bf16[512,640]{1,0:T(8,128)(2,1)S(1)}, bf16[512,640]{1,0:T(8,128)(2,1)S(1)}, u32[]{:S(2)}, u32[]{:S(2)}) collective-permute-start(bf16[512,640]{1,0:T(8,128)(2,1)S(1)} %get-tuple-element.19), channel_id=1, source_target_pairs={{0,2},{1,3},{2,0},{3,1},{4,6},{5,7},{6,4},{7,5},{8,10},{9,11},{10,... | collective-permute-start | bytes 1966088 | tf_op jit(solution)/shard_map/ppermute | solution.py:268
  338.0 84.4 %collective-permute-start.12 = (bf16[512,640]{1,0:T(8,128)(2,1)S(1)}, bf16[512,640]{1,0:T(8,128)(2,1)S(1)}, u32[]{:S(2)}, u32[]{:S(2)}) collective-permute-start(bf16[512,640]{1,0:T(8,128)(2,1)S(1)} %copy-done.3), channel_id=1, source_target_pairs={{0,2},{1,3},{2,0},{3,1},{4,6},{5,7},{6,4},{7,5},{8,10},{9,11},{10,... | collective-permute-start | bytes 1966088 | tf_op jit(solution)/shard_map/ppermute | solution.py:268
  340.4 57.7 %collective-permute-start.11 = (bf16[512,640]{1,0:T(8,128)(2,1)S(1)}, bf16[512,640]{1,0:T(8,128)(2,1)S(1)}, u32[]{:S(2)}, u32[]{:S(2)}) collective-permute-start(bf16[512,640]{1,0:T(8,128)(2,1)S(1)} %get-tuple-element.19), channel_id=1, source_target_pairs={{0,1},{1,2},{2,3},{3,0},{4,5},{5,6},{6,7},{7,4},{8,9},{9,10},{10,1... | collective-permute-start | bytes 1966088 | tf_op jit(solution)/shard_map/ppermute | solution.py:268
  394.5 30.8 %collective-permute-start.10 = (bf16[512,640]{1,0:T(8,128)(2,1)S(1)}, bf16[512,640]{1,0:T(8,128)(2,1)S(1)}, u32[]{:S(2)}, u32[]{:S(2)}) collective-permute-start(bf16[512,640]{1,0:T(8,128)(2,1)S(1)} %copy-done.3), channel_id=1, source_target_pairs={{0,1},{1,2},{2,3},{3,0},{4,5},{5,6},{6,7},{7,4},{8,9},{9,10},{10,1... | collective-permute-start | bytes 1966088 | tf_op jit(solution)/shard_map/ppermute | solution.py:268
  (17 other events, 133.5 us)
Sparse Core Ops, SparseCore 0:
  10.7 88.3 all-gather.7
  101.0 58.1 all-gather.3
  161.1 74.1 all-gather.5
where the time goes:
time: 443 us; the launch traced here: 435 us
  waiting for transfers between devices  184 us (42%)
  starting transfers between devices  80.8 us (18%)
  matrix products  70.1 us (16%)
  Pallas kernels  37.5 us (8%)
  other arithmetic  24.9 us (6%)
  local copies, waits for them, and re-layouts  22.7 us (5%)
  between operations  14.7 us (3%)
    ppermute x12, waiting for transfers between devices, layer(): lax.ppermute(attended, 'mp', [(i, (i + s) % planes) for i in range(planes)])  110 us
    ppermute x12, starting transfers between devices, layer(): lax.ppermute(attended, 'mp', [(i, (i + s) % planes) for i in range(planes)])  61.3 us
    ppermute x10, waiting for transfers between devices, exchange(): lax.ppermute(piece, axis, [(i, (i + s) % size) for i in range(size)])  50.4 us
    dot_general x4, matrix products, layer(): jnp.dot(normed[rows], gathered[g], preferred_element_type=jnp.float32)  45.7 us
    pallas_call x4, Pallas kernels, attention(): pl.pallas_call(functools.partial(attention_kernel, block, prev_len), grid...  37.5 us
    dot_general x16, matrix products, layer(): jnp.dot(held[s][r][g], weights[s][g * width_q:(g + 1) * width_q], preferr...  24.4 us
    all_to_all x1, waiting for transfers between devices, layer(): lax.all_to_all(outgoing, 'dp', split_axis=1, concat_axis=1, tiled=True)  24.3 us
    ppermute x10, starting transfers between devices, exchange(): lax.ppermute(piece, axis, [(i, (i + s) % size) for i in range(size)])  14.3 us
  transfers between devices with their start and end apart: 26, of which 13 were waited for; matrix products, arithmetic and copies ran while one was open for 25% of the time, Pallas kernels for 9%

commit v1 on v0

--- a/solution.py
+++ b/solution.py
@@ -264,14 +264,13 @@
                 )
             held[0][r].append(attended)
             for s in range(1, planes):
-                held[s][r].append(
-                    lax.ppermute(
-                        attended, "mp", [(i, (i + s) % planes) for i in range(planes)]
-                    )
-                )
+                high = 1 << (s.bit_length() - 1)
+                low = s - high
+                _, moved, step = ("relay", held[high][r][g], low) if low else ("send", attended, s)
+                held[s][r].append(lax.ppermute(moved, "mp", [(i, i ^ step) for i in range(planes)]))
     weights = []
     for s in range(planes):
-        source = lax.rem(my_plane - s + planes, planes)
+        source = my_plane ^ s
         rows_of = lax.dynamic_index_in_dim(out_weight, source, axis=1, keepdims=False)
         weights.append(rows_of.reshape(-1, out_cols))
     outputs = []

time: 443 us -> 401 us (0.905)
  starting transfers between devices: 80.8 us -> 40.8 us
    ppermute x12, starting transfers between devices: 61.3 us -> 21.3 us  [layer(): lax.ppermute(moved, 'mp', [(i, i ^ step) for i in range(planes)])]
  transfers between devices with their start and end apart: 26 -> 26, of which waited for: 13 -> 16; matrix products, arithmetic and copies ran while one was open for 25% -> 27% of each run, Pallas kernels for 9% -> 10%
where the time goes in v1:
time: 401 us; the launch traced here: 394 us
  waiting for transfers between devices  184 us (46%)
  matrix products  69.1 us (17%)
  starting transfers between devices  40.8 us (10%)
  Pallas kernels  37.6 us (9%)
  other arithmetic  24.9 us (6%)
  local copies, waits for them, and re-layouts  22.6 us (6%)
  between operations  14.9 us (4%)
    ppermute x12, waiting for transfers between devices, layer(): lax.ppermute(moved, 'mp', [(i, i ^ step) for i in range(planes)])  109 us
    ppermute x10, waiting for transfers between devices, exchange(): lax.ppermute(piece, axis, [(i, (i + s) % size) for i in range(size)])  50.4 us
    dot_general x4, matrix products, layer(): jnp.dot(normed[rows], gathered[g], preferred_element_type=jnp.float32)  45.5 us
    pallas_call x4, Pallas kernels, attention(): pl.pallas_call(functools.partial(attention_kernel, block, prev_len), grid...  37.6 us
    all_to_all x1, waiting for transfers between devices, layer(): lax.all_to_all(outgoing, 'dp', split_axis=1, concat_axis=1, tiled=True)  24.3 us
    dot_general x16, matrix products, layer(): jnp.dot(held[s][r][g], weights[s][g * width_q:(g + 1) * width_q], preferr...  23.6 us
    ppermute x12, starting transfers between devices, layer(): lax.ppermute(moved, 'mp', [(i, i ^ step) for i in range(planes)])  21.3 us
    ppermute x10, starting transfers between devices, exchange(): lax.ppermute(piece, axis, [(i, (i + s) % size) for i in range(size)])  14.3 us
  transfers between devices with their start and end apart: 26, of which 16 were waited for; matrix products, arithmetic and copies ran while one was open for 27% of the time, Pallas kernels for 10%

profile of v1, /device:TPU:0, one launch (start us, length us, event | category | flops | bytes accessed | tf_op | source)
XLA Modules:
  0.0 393.7 jit_solution(12042377844723343208)
XLA Ops:
  24.1 24.3 %all-to-all-done = bf16[2,8,2,64,256]{4,3,2,0,1:T(8,128)(2,1)S(1)} async-done(((bf16[2,8,2,64,256]{4,3,2,0,1:T(8,128)(2,1)}), bf16[2,8,2,64,256]{4,3,2,0,1:T(8,128)(2,1)S(1)}, u32[]{:S(2)}, u32[]{:S(2)}) %all-to-all-start) | async-done | bytes 1048608 | tf_op jit(solution)/shard_map/all_to_all | solution.py:223
  54.1 6.8 %collective-permute-done = bf16[160,640]{1,0:T(8,128)(2,1)S(1)} collective-permute-done((bf16[160,640]{1,0:T(8,128)(2,1)}, bf16[160,640]{1,0:T(8,128)(2,1)S(1)}, u32[]{:S(2)}, u32[]{:S(2)}) %collective-permute-start) | collective-permute-done | bytes 204832 | tf_op jit(solution)/shard_map/ppermute | solution.py:152
  63.2 5.8 %collective-permute-start.6 = (bf16[160,640]{1,0:T(8,128)(2,1)S(1)}, bf16[160,640]{1,0:T(8,128)(2,1)S(1)}, u32[]{:S(2)}, u32[]{:S(2)}) collective-permute-start(bf16[160,640]{1,0:T(8,128)(2,1)S(1)} %get-tuple-element.67), channel_id=1, source_target_pairs={{0,28},{4,0},{8,4},{12,8},{16,12},{20,16},{24,20},{28,24},{1,29},{... | collective-permute-start | bytes 614408 | tf_op jit(solution)/shard_map/ppermute | solution.py:152
  72.6 7.1 %collective-permute-done.4 = bf16[160,640]{1,0:T(8,128)(2,1)S(1)} collective-permute-done((bf16[160,640]{1,0:T(8,128)(2,1)}, bf16[160,640]{1,0:T(8,128)(2,1)S(1)}, u32[]{:S(2)}, u32[]{:S(2)}) %collective-permute-start.4) | collective-permute-done | bytes 204832 | tf_op jit(solution)/shard_map/ppermute | solution.py:152
  92.3 6.7 %collective-permute-done.7 = bf16[160,1280]{1,0:T(8,128)(2,1)S(1)} collective-permute-done((bf16[160,1280]{1,0:T(8,128)(2,1)}, bf16[160,1280]{1,0:T(8,128)(2,1)S(1)}, u32[]{:S(2)}, u32[]{:S(2)}) %collective-permute-start.7) | collective-permute-done | bytes 409632 | tf_op jit(solution)/shard_map/ppermute | solution.py:152
  99.8 19.0 %collective-permute-done.8 = bf16[160,1280]{1,0:T(8,128)(2,1)S(1)} collective-permute-done((bf16[160,1280]{1,0:T(8,128)(2,1)S(1)}, bf16[160,1280]{1,0:T(8,128)(2,1)S(1)}, u32[]{:S(2)}, u32[]{:S(2)}) %collective-permute-start.8) | collective-permute-done | bytes 409632 | tf_op jit(solution)/shard_map/ppermute | solution.py:152
  124.5 6.1 %fusion = f32[1024]{0:T(1024)S(1)} fusion(bf16[1024,5120]{1,0:T(8,128)(2,1)} %param.14), kind=kLoop, calls=%fused_computation.6 | loop fusion | flops 15727616 | bytes 10489856 | tf_op jit(solution)/shard_map/reduce_sum | solution.py:24
  130.6 11.6 %fusion.2 = bf16[1024,5120]{1,0:T(8,128)(2,1)} fusion(bf16[1024,5120]{1,0:T(8,128)(2,1)} %param.14, f32[5120]{0:T(1024)S(1)} %convert_element_type.91, f32[1024]{0:T(1024)S(1)} %add_rsqrt_fusion), kind=kLoop, calls=%fused_computation.8 | loop fusion | flops 20971520 | bytes 20996096 | tf_op jit(solution)/shard_map/convert_element_type | solution.py:25
  142.2 12.3 %fusion.38.refs_0_.refs_1_.refs_2_ = f32[512,896]{1,0:T(8,128)S(1)} fusion(bf16[5120,896]{1,0:T(8,128)(2,1)} %all-gather.8.cloned.1.call-done, bf16[1024,5120]{1,0:T(8,128)(2,1)} %fusion.2, f32[896]{0:T(1024)S(1)} %maximum_convert_fusion.1), kind=kOutput, calls=%fused_computation.51 | convolution fusion | flops 4698079232 | bytes 16256512 | tf_op jit(solution)/shard_map/dot_general | solution.py:252
  154.5 8.2 %shard_map.119 = (bf16[512,640]{1,0:T(8,128)(2,1)S(1)}, bf16[512,128]{1,0:T(8,128)(2,1)S(1)}, bf16[512,128]{1,0:T(8,128)(2,1)S(1)}) custom-call(f32[512,896]{1,0:T(8,128)S(1)} %fusion.38.refs_0_.refs_1_.refs_2_, f32[512,896]{1,0:T(8,128)S(1)} %fusion.38.refs_0_.refs_1_.refs_2_, f32[512,896]{1,0:T(8,128)S(1)} %fusion.38.refs_0_.refs_1_.refs_2_, ...), custom_call_target="tpu_custom_call" | custom-call | flops 4026531840 | bytes 2752512 | tf_op jit(solution)/shard_map/pallas_call | solution.py:113
  162.7 10.8 %fusion.44.refs_0_.refs_1_.refs_2_ = f32[512,896]{1,0:T(8,128)S(1)} fusion(bf16[5120,896]{1,0:T(8,128)(2,1)} %all-gather.8.cloned.1.call-done, bf16[1024,5120]{1,0:T(8,128)(2,1)S(1)} %copy-done.5, f32[896]{0:T(1024)S(1)} %maximum_convert_fusion.1), kind=kOutput, calls=%fused_computation.53 | convolution fusion | flops 4698079232 | bytes 16257024 | tf_op jit(solution)/shard_map/dot_general | solution.py:252
  173.5 10.7 %shard_map.121 = (bf16[512,640]{1,0:T(8,128)(2,1)S(1)}, bf16[512,128]{1,0:T(8,128)(2,1)}, bf16[512,128]{1,0:T(8,128)(2,1)}) custom-call(f32[512,896]{1,0:T(8,128)S(1)} %fusion.44.refs_0_.refs_1_.refs_2_, f32[512,896]{1,0:T(8,128)S(1)} %fusion.44.refs_0_.refs_1_.refs_2_, f32[512,896]{1,0:T(8,128)S(1)} %fusion.44.refs_0_.refs_1_.refs_2_, ...), custom_call_target="tpu_custom_call" | custom-call | flops 5368709120 | bytes 2752512 | tf_op jit(solution)/shard_map/pallas_call | solution.py:113
  184.2 9.5 %collective-permute-start.19 = (bf16[512,640]{1,0:T(8,128)(2,1)S(1)}, bf16[512,640]{1,0:T(8,128)(2,1)}, u32[]{:S(2)}, u32[]{:S(2)}) collective-permute-start(bf16[512,640]{1,0:T(8,128)(2,1)S(1)} %get-tuple-element.25), channel_id=1, source_target_pairs={{0,2},{1,3},{2,0},{3,1},{4,6},{5,7},{6,4},{7,5},{8,10},{9,11},{10,... | collective-permute-start | bytes 1966088 | tf_op jit(solution)/shard_map/ppermute | solution.py:270
  194.5 14.4 %fusion.35.refs_0_.refs_1_.refs_2_ = f32[512,896]{1,0:T(8,128)S(1)} fusion(bf16[5120,896]{1,0:T(8,128)(2,1)} %all-gather.4.cloned.1.call-done, bf16[1024,5120]{1,0:T(8,128)(2,1)} %fusion.2, f32[896]{0:T(1024)S(1)} %maximum_convert_fusion), kind=kOutput, calls=%fused_computation.50 | convolution fusion | flops 4698079232 | bytes 16256512 | tf_op jit(solution)/shard_map/dot_general | solution.py:252
  208.9 8.2 %shard_map.118 = (bf16[512,640]{1,0:T(8,128)(2,1)S(1)}, bf16[512,128]{1,0:T(8,128)(2,1)S(1)}, bf16[512,128]{1,0:T(8,128)(2,1)S(1)}) custom-call(f32[512,896]{1,0:T(8,128)S(1)} %fusion.35.refs_0_.refs_1_.refs_2_, f32[512,896]{1,0:T(8,128)S(1)} %fusion.35.refs_0_.refs_1_.refs_2_, f32[512,896]{1,0:T(8,128)S(1)} %fusion.35.refs_0_.refs_1_.refs_2_, ...), custom_call_target="tpu_custom_call" | custom-call | flops 4026531840 | bytes 2752512 | tf_op jit(solution)/shard_map/pallas_call | solution.py:113
  217.1 7.9 %fusion.41.refs_0_.refs_1_.refs_2_ = f32[512,896]{1,0:T(8,128)S(1)} fusion(bf16[5120,896]{1,0:T(8,128)(2,1)S(1)} %copy-done.13, bf16[1024,5120]{1,0:T(8,128)(2,1)} %fusion.2, f32[896]{0:T(1024)S(1)} %maximum_convert_fusion), kind=kOutput, calls=%fused_computation.52 | convolution fusion | flops 4698079232 | bytes 16256512 | tf_op jit(solution)/shard_map/dot_general | solution.py:252
  225.1 10.5 %shard_map.120 = (bf16[512,640]{1,0:T(8,128)(2,1)}, bf16[512,128]{1,0:T(8,128)(2,1)}, bf16[512,128]{1,0:T(8,128)(2,1)}) custom-call(f32[512,896]{1,0:T(8,128)S(1)} %fusion.41.refs_0_.refs_1_.refs_2_, f32[512,896]{1,0:T(8,128)S(1)} %fusion.41.refs_0_.refs_1_.refs_2_, f32[512,896]{1,0:T(8,128)S(1)} %fusion.41.refs_0_.refs_1_.refs_2_, ...), custom_call_target="tpu_custom_call" | custom-call | flops 5368709120 | bytes 2752512 | tf_op jit(solution)/shard_map/pallas_call | solution.py:113
  239.5 5.7 %constant_dynamic-slice_fusion = (bf16[4,1,160,1280]{3,2,1,0:T(8,128)(2,1)S(1)}, bf16[4,1,160,1280]{3,2,1,0:T(8,128)(2,1)S(1)}, bf16[4,1,160,1280]{3,2,1,0:T(8,1...) fusion(bf16[8,4,160,1280]{3,2,1,0:T(8,128)(2,1)} %bitcast.89, ...), kind=kLoop, calls=%fused_computation.74 | loop fusion | bytes 26214420 | tf_op jit(solution)/shard_map/slice | solution.py:284
  254.0 14.8 %collective-permute-done.18 = bf16[512,640]{1,0:T(8,128)(2,1)S(1)} collective-permute-done((bf16[512,640]{1,0:T(8,128)(2,1)}, bf16[512,640]{1,0:T(8,128)(2,1)S(1)}, u32[]{:S(2)}, u32[]{:S(2)}) %collective-permute-start.18) | collective-permute-done | bytes 655392 | tf_op jit(solution)/shard_map/ppermute | solution.py:270
  274.4 34.3 %collective-permute-done.21 = bf16[512,640]{1,0:T(8,128)(2,1)S(1)} collective-permute-done((bf16[512,640]{1,0:T(8,128)(2,1)}, bf16[512,640]{1,0:T(8,128)(2,1)S(1)}, u32[]{:S(2)}, u32[]{:S(2)}) %collective-permute-start.21) | collective-permute-done | bytes 655392 | tf_op jit(solution)/shard_map/ppermute | solution.py:270
  314.4 9.7 %collective-permute-done.12 = bf16[512,640]{1,0:T(8,128)(2,1)S(1)} collective-permute-done((bf16[512,640]{1,0:T(8,128)(2,1)S(1)}, bf16[512,640]{1,0:T(8,128)(2,1)S(1)}, u32[]{:S(2)}, u32[]{:S(2)}) %collective-permute-start.12) | collective-permute-done | bytes 655392 | tf_op jit(solution)/shard_map/ppermute | solution.py:270
  325.4 17.2 %collective-permute-done.20 = bf16[512,640]{1,0:T(8,128)(2,1)S(1)} collective-permute-done((bf16[512,640]{1,0:T(8,128)(2,1)S(1)}, bf16[512,640]{1,0:T(8,128)(2,1)S(1)}, u32[]{:S(2)}, u32[]{:S(2)}) %collective-permute-start.20) | collective-permute-done | bytes 655392 | tf_op jit(solution)/shard_map/ppermute | solution.py:270
  348.5 22.2 %collective-permute-done.15 = bf16[512,640]{1,0:T(8,128)(2,1)S(1)} collective-permute-done((bf16[512,640]{1,0:T(8,128)(2,1)}, bf16[512,640]{1,0:T(8,128)(2,1)S(1)}, u32[]{:S(2)}, u32[]{:S(2)}) %collective-permute-start.15) | collective-permute-done | bytes 655392 | tf_op jit(solution)/shard_map/ppermute | solution.py:270
  373.1 10.8 %collective-permute-done.14 = bf16[512,640]{1,0:T(8,128)(2,1)S(1)} collective-permute-done((bf16[512,640]{1,0:T(8,128)(2,1)S(1)}, bf16[512,640]{1,0:T(8,128)(2,1)S(1)}, u32[]{:S(2)}, u32[]{:S(2)}) %collective-permute-start.14) | collective-permute-done | bytes 655392 | tf_op jit(solution)/shard_map/ppermute | solution.py:270
  (150 shorter events, 84.0 us)
Async XLA Ops:
  6.5 135.6 %all-gather.8.cloned.1.call-start = ((), (), s32[]{:S(2)}) async-start(), calls=%async_computation.3 | async-start | bytes 10321920 | tf_op jit(solution)/shard_map/all_gather | solution.py:196
  10.5 184.0 %all-gather.4.cloned.1.call-start = ((), (), s32[]{:S(2)}) async-start(), calls=%async_computation.1 | async-start | bytes 10321920 | tf_op jit(solution)/shard_map/all_gather | solution.py:196
  18.8 29.7 %all-to-all-start = ((bf16[2,8,2,64,256]{4,3,2,0,1:T(8,128)(2,1)}), bf16[2,8,2,64,256]{4,3,2,0,1:T(8,128)(2,1)S(1)}, u32[]{:S(2)}, u32[]{:S(2)}) async-start(bf16[2,8,2,64,256]{4,3,2,0,1:T(8,128)(2,1)} %copy.42), calls=%async_computation | async-start | bytes 2097152 | tf_op jit(solution)/shard_map/all_to_all | solution.py:223
  24.0 215.6 %all-gather.6.cloned.1.call-start = ((), (), s32[]{:S(2)}) async-start(), calls=%async_computation.2 | async-start | bytes 14745600 | tf_op jit(solution)/shard_map/all_gather | solution.py:239
  50.8 12.4 %collective-permute-start.1 = (bf16[160,640]{1,0:T(8,128)(2,1)}, bf16[160,640]{1,0:T(8,128)(2,1)S(1)}, u32[]{:S(2)}, u32[]{:S(2)}) collective-permute-start(bf16[160,640]{1,0:T(8,128)(2,1)} %get-tuple-element.72), channel_id=1, source_target_pairs={{0,8},{4,12},{8,16},{12,20},{16,24},{20,28},{24,0},{28,4},{1,9},{5... | collective-permute-start | bytes 614408 | tf_op jit(solution)/shard_map/ppermute | solution.py:152
  50.9 21.5 %collective-permute-start.2 = (bf16[160,640]{1,0:T(8,128)(2,1)}, bf16[160,640]{1,0:T(8,128)(2,1)S(1)}, u32[]{:S(2)}, u32[]{:S(2)}) collective-permute-start(bf16[160,640]{1,0:T(8,128)(2,1)} %get-tuple-element.71), channel_id=1, source_target_pairs={{0,12},{4,16},{8,20},{12,24},{16,28},{20,0},{24,4},{28,8},{1,13},{... | collective-permute-start | bytes 614408 | tf_op jit(solution)/shard_map/ppermute | solution.py:152
  52.9 19.7 %collective-permute-start.3 = (bf16[160,640]{1,0:T(8,128)(2,1)}, bf16[160,640]{1,0:T(8,128)(2,1)S(1)}, u32[]{:S(2)}, u32[]{:S(2)}) collective-permute-start(bf16[160,640]{1,0:T(8,128)(2,1)} %get-tuple-element.70), channel_id=1, source_target_pairs={{0,16},{4,20},{8,24},{12,28},{16,0},{20,4},{24,8},{28,12},{1,17},{... | collective-permute-start | bytes 614408 | tf_op jit(solution)/shard_map/ppermute | solution.py:152
  54.1 25.6 %collective-permute-start.4 = (bf16[160,640]{1,0:T(8,128)(2,1)}, bf16[160,640]{1,0:T(8,128)(2,1)S(1)}, u32[]{:S(2)}, u32[]{:S(2)}) collective-permute-start(bf16[160,640]{1,0:T(8,128)(2,1)} %get-tuple-element.69), channel_id=1, source_target_pairs={{0,20},{4,24},{8,28},{12,0},{16,4},{20,8},{24,12},{28,16},{1,21},{... | collective-permute-start | bytes 614408 | tf_op jit(solution)/shard_map/ppermute | solution.py:152
  60.9 19.0 %collective-permute-start.5 = (bf16[160,640]{1,0:T(8,128)(2,1)S(1)}, bf16[160,640]{1,0:T(8,128)(2,1)S(1)}, u32[]{:S(2)}, u32[]{:S(2)}) collective-permute-start(bf16[160,640]{1,0:T(8,128)(2,1)S(1)} %get-tuple-element.68), channel_id=1, source_target_pairs={{0,24},{4,28},{8,0},{12,4},{16,8},{20,12},{24,16},{28,20},{1,25},{... | collective-permute-start | bytes 614408 | tf_op jit(solution)/shard_map/ppermute | solution.py:152
  63.2 21.5 %collective-permute-start.6 = (bf16[160,640]{1,0:T(8,128)(2,1)S(1)}, bf16[160,640]{1,0:T(8,128)(2,1)S(1)}, u32[]{:S(2)}, u32[]{:S(2)}) collective-permute-start(bf16[160,640]{1,0:T(8,128)(2,1)S(1)} %get-tuple-element.67), channel_id=1, source_target_pairs={{0,28},{4,0},{8,4},{12,8},{16,12},{20,16},{24,20},{28,24},{1,29},{... | collective-permute-start | bytes 614408 | tf_op jit(solution)/shard_map/ppermute | solution.py:152
  88.4 30.4 %collective-permute-start.8 = (bf16[160,1280]{1,0:T(8,128)(2,1)S(1)}, bf16[160,1280]{1,0:T(8,128)(2,1)S(1)}, u32[]{:S(2)}, u32[]{:S(2)}) collective-permute-start(bf16[160,1280]{1,0:T(8,128)(2,1)S(1)} %get-tuple-element.64), channel_id=1, source_target_pairs={{0,2},{1,3},{2,0},{3,1},{4,6},{5,7},{6,4},{7,5},{8,10},{9,11},{10,... | collective-permute-start | bytes 1228808 | tf_op jit(solution)/shard_map/ppermute | solution.py:152
  90.8 28.8 %collective-permute-start.9 = (bf16[160,1280]{1,0:T(8,128)(2,1)S(1)}, bf16[160,1280]{1,0:T(8,128)(2,1)S(1)}, u32[]{:S(2)}, u32[]{:S(2)}) collective-permute-start(bf16[160,1280]{1,0:T(8,128)(2,1)S(1)} %get-tuple-element.63), channel_id=1, source_target_pairs={{0,3},{1,0},{2,1},{3,2},{4,7},{5,4},{6,5},{7,6},{8,11},{9,8},{10,9... | collective-permute-start | bytes 1228808 | tf_op jit(solution)/shard_map/ppermute | solution.py:152
  184.2 66.9 %collective-permute-start.19 = (bf16[512,640]{1,0:T(8,128)(2,1)S(1)}, bf16[512,640]{1,0:T(8,128)(2,1)}, u32[]{:S(2)}, u32[]{:S(2)}) collective-permute-start(bf16[512,640]{1,0:T(8,128)(2,1)S(1)} %get-tuple-element.25), channel_id=1, source_target_pairs={{0,2},{1,3},{2,0},{3,1},{4,6},{5,7},{6,4},{7,5},{8,10},{9,11},{10,... | collective-permute-start | bytes 1966088 | tf_op jit(solution)/shard_map/ppermute | solution.py:270
  193.7 76.3 %collective-permute-start.17 = (bf16[512,640]{1,0:T(8,128)(2,1)S(1)}, bf16[512,640]{1,0:T(8,128)(2,1)}, u32[]{:S(2)}, u32[]{:S(2)}) collective-permute-start(bf16[512,640]{1,0:T(8,128)(2,1)S(1)} %get-tuple-element.25), channel_id=1, source_target_pairs={{0,1},{1,0},{2,3},{3,2},{4,5},{5,4},{6,7},{7,6},{8,9},{9,8},{10,11... | collective-permute-start | bytes 1966088 | tf_op jit(solution)/shard_map/ppermute | solution.py:270
  235.6 33.2 %collective-permute-start.18 = (bf16[512,640]{1,0:T(8,128)(2,1)}, bf16[512,640]{1,0:T(8,128)(2,1)S(1)}, u32[]{:S(2)}, u32[]{:S(2)}) collective-permute-start(bf16[512,640]{1,0:T(8,128)(2,1)} %get-tuple-element.22), channel_id=1, source_target_pairs={{0,2},{1,3},{2,0},{3,1},{4,6},{5,7},{6,4},{7,5},{8,10},{9,11},{10,... | collective-permute-start | bytes 1966088 | tf_op jit(solution)/shard_map/ppermute | solution.py:270
  237.1 75.2 %collective-permute-start.16 = (bf16[512,640]{1,0:T(8,128)(2,1)}, bf16[512,640]{1,0:T(8,128)(2,1)S(1)}, u32[]{:S(2)}, u32[]{:S(2)}) collective-permute-start(bf16[512,640]{1,0:T(8,128)(2,1)} %get-tuple-element.22), channel_id=1, source_target_pairs={{0,1},{1,0},{2,3},{3,2},{4,5},{5,4},{6,7},{7,6},{8,9},{9,8},{10,11... | collective-permute-start | bytes 1966088 | tf_op jit(solution)/shard_map/ppermute | solution.py:270
  237.1 75.3 %collective-permute-start.13 = (bf16[512,640]{1,0:T(8,128)(2,1)S(1)}, bf16[512,640]{1,0:T(8,128)(2,1)}, u32[]{:S(2)}, u32[]{:S(2)}) collective-permute-start(bf16[512,640]{1,0:T(8,128)(2,1)S(1)} %get-tuple-element.19), channel_id=1, source_target_pairs={{0,2},{1,3},{2,0},{3,1},{4,6},{5,7},{6,4},{7,5},{8,10},{9,11},{10,... | collective-permute-start | bytes 1966088 | tf_op jit(solution)/shard_map/ppermute | solution.py:270
  251.2 72.9 %collective-permute-start.12 = (bf16[512,640]{1,0:T(8,128)(2,1)S(1)}, bf16[512,640]{1,0:T(8,128)(2,1)S(1)}, u32[]{:S(2)}, u32[]{:S(2)}) collective-permute-start(bf16[512,640]{1,0:T(8,128)(2,1)S(1)} %copy-done.3), channel_id=1, source_target_pairs={{0,2},{1,3},{2,0},{3,1},{4,6},{5,7},{6,4},{7,5},{8,10},{9,11},{10,... | collective-permute-start | bytes 1966088 | tf_op jit(solution)/shard_map/ppermute | solution.py:270
  268.8 40.0 %collective-permute-start.21 = (bf16[512,640]{1,0:T(8,128)(2,1)}, bf16[512,640]{1,0:T(8,128)(2,1)S(1)}, u32[]{:S(2)}, u32[]{:S(2)}) collective-permute-start(bf16[512,640]{1,0:T(8,128)(2,1)} %collective-permute-done.19), channel_id=1, source_target_pairs={{0,1},{1,0},{2,3},{3,2},{4,5},{5,4},{6,7},{7,6},{8,9},{9,8},{10,11... | collective-permute-start | bytes 1966088 | tf_op jit(solution)/shard_map/ppermute | solution.py:270
  270.0 77.3 %collective-permute-start.11 = (bf16[512,640]{1,0:T(8,128)(2,1)S(1)}, bf16[512,640]{1,0:T(8,128)(2,1)S(1)}, u32[]{:S(2)}, u32[]{:S(2)}) collective-permute-start(bf16[512,640]{1,0:T(8,128)(2,1)S(1)} %get-tuple-element.19), channel_id=1, source_target_pairs={{0,1},{1,0},{2,3},{3,2},{4,5},{5,4},{6,7},{7,6},{8,9},{9,8},{10,11... | collective-permute-start | bytes 1966088 | tf_op jit(solution)/shard_map/ppermute | solution.py:270
  308.7 33.9 %collective-permute-start.20 = (bf16[512,640]{1,0:T(8,128)(2,1)S(1)}, bf16[512,640]{1,0:T(8,128)(2,1)S(1)}, u32[]{:S(2)}, u32[]{:S(2)}) collective-permute-start(bf16[512,640]{1,0:T(8,128)(2,1)S(1)} %collective-permute-done.18), channel_id=1, source_target_pairs={{0,1},{1,0},{2,3},{3,2},{4,5},{5,4},{6,7},{7,6},{8,9},{9,8},{10,11... | collective-permute-start | bytes 1966088 | tf_op jit(solution)/shard_map/ppermute | solution.py:270
  312.3 59.6 %collective-permute-start.10 = (bf16[512,640]{1,0:T(8,128)(2,1)S(1)}, bf16[512,640]{1,0:T(8,128)(2,1)S(1)}, u32[]{:S(2)}, u32[]{:S(2)}) collective-permute-start(bf16[512,640]{1,0:T(8,128)(2,1)S(1)} %copy-done.3), channel_id=1, source_target_pairs={{0,1},{1,0},{2,3},{3,2},{4,5},{5,4},{6,7},{7,6},{8,9},{9,8},{10,11... | collective-permute-start | bytes 1966088 | tf_op jit(solution)/shard_map/ppermute | solution.py:270
  312.4 58.3 %collective-permute-start.15 = (bf16[512,640]{1,0:T(8,128)(2,1)}, bf16[512,640]{1,0:T(8,128)(2,1)S(1)}, u32[]{:S(2)}, u32[]{:S(2)}) collective-permute-start(bf16[512,640]{1,0:T(8,128)(2,1)} %collective-permute-done.13), channel_id=1, source_target_pairs={{0,1},{1,0},{2,3},{3,2},{4,5},{5,4},{6,7},{7,6},{8,9},{9,8},{10,11... | collective-permute-start | bytes 1966088 | tf_op jit(solution)/shard_map/ppermute | solution.py:270
  324.1 59.7 %collective-permute-start.14 = (bf16[512,640]{1,0:T(8,128)(2,1)S(1)}, bf16[512,640]{1,0:T(8,128)(2,1)S(1)}, u32[]{:S(2)}, u32[]{:S(2)}) collective-permute-start(bf16[512,640]{1,0:T(8,128)(2,1)S(1)} %collective-permute-done.12), channel_id=1, source_target_pairs={{0,1},{1,0},{2,3},{3,2},{4,5},{5,4},{6,7},{7,6},{8,9},{9,8},{10,11... | collective-permute-start | bytes 1966088 | tf_op jit(solution)/shard_map/ppermute | solution.py:270
  (17 other events, 133.1 us)
Sparse Core Ops, SparseCore 0:
  10.7 88.3 all-gather.7
  101.0 58.1 all-gather.3
  161.1 74.2 all-gather.5
